TPU v7x, 256 devices: a whole 4x4x8 slice. The times are simulated.
256 devices in a mesh: alpha: 8 (over z_lo, y), beta: 32 (over z_hi, x, core).
Axes of the slice: x: 4, y: 4, z: 8 (z_hi: 4, z_lo: 2; z = z_hi * 2 + z_lo), core: 2. Of those that a mesh axis runs over, the one named last changes fastest.
Arguments:
- ci_vectors: bfloat16 [8, 4096, 4096], P(None, 'alpha', 'beta'), may hold values from -6 to 6
- alpha_blocks: bfloat16 [32, 16, 128, 128], P('alpha'), may hold values from -0.125 to 0.125
- alpha_cols: int32 [32, 16], P('alpha'), may hold values from 0 to 31, all different within a row
- beta_blocks: bfloat16 [32, 16, 128, 128], P('beta'), may hold values from -0.125 to 0.125
- beta_cols: int32 [32, 16], P('beta'), may hold values from 0 to 31, all different within a row
- diagonal: float32 [4096, 4096], P('alpha', 'beta'), may hold values from -1 to 3
Outputs:
- sigma_vectors: bfloat16 [8, 4096, 4096], P(None, 'alpha', 'beta')
Inputs may be any that keep to these rules, and one draw needn't show every extreme that they name: `alpha_cols`: each block-row names 16 different block-columns. `beta_cols`: each block-row names 16 different block-columns.
All inputs are finite; a program needn't handle non-finite values.
Results may differ from a plain program's by a relative error of at most 0.001.
Values may be sent and summed in bfloat16 or wider, within the bound.
A program may use at most 128 MiB of HBM per device.

v0:
```python
import jax
import jax.numpy as jnp
from jax import lax
from jax.sharding import PartitionSpec as P


def alpha_pass(ci_vectors, alpha_blocks, alpha_cols):
    vectors, rows_local, cols_local = ci_vectors.shape
    block = alpha_blocks.shape[-1]
    owned = alpha_blocks.shape[0]
    whole = lax.all_gather(ci_vectors, "alpha", axis=1, tiled=True)
    grid = whole.reshape(vectors, whole.shape[1] // block, block, cols_local)
    picked = grid[:, alpha_cols]
    term = jnp.einsum("rkij,vrkjb->vrib", alpha_blocks, picked, preferred_element_type=jnp.float32)
    return term.reshape(vectors, owned * block, cols_local)


def beta_pass(ci_vectors, beta_blocks, beta_cols):
    vectors, rows_local, cols_local = ci_vectors.shape
    block = beta_blocks.shape[-1]
    turned = lax.all_to_all(ci_vectors, "beta", split_axis=1, concat_axis=2, tiled=True)
    few_rows = turned.shape[1]
    all_cols = turned.shape[2]
    grid = turned.reshape(vectors, few_rows, all_cols // block, block)
    hb_piece = lax.all_gather(beta_blocks, "beta", axis=0, tiled=True)
    col_piece = lax.all_gather(beta_cols.astype(jnp.bfloat16), "beta", axis=0, tiled=True)
    columns = col_piece.astype(jnp.int32)
    count = hb_piece.shape[0]
    picked = grid[:, :, columns]
    term = jnp.einsum("vtnkj,nkij->vtni", picked, hb_piece, preferred_element_type=jnp.float32)
    updated = term.reshape(vectors, few_rows, count * block)
    return lax.all_to_all(updated, "beta", split_axis=2, concat_axis=1, tiled=True)


def shards(ci_vectors, alpha_blocks, alpha_cols, beta_blocks, beta_cols, diagonal):
    alpha_part = alpha_pass(ci_vectors, alpha_blocks, alpha_cols)
    beta_part = beta_pass(ci_vectors, beta_blocks, beta_cols)
    total = alpha_part + beta_part + diagonal[None, :, :] * ci_vectors.astype(jnp.float32)
    return total.astype(jnp.bfloat16)


def solution(mesh):
    placed = (
        P(None, "alpha", "beta"),
        P("alpha", None, None, None),
        P("alpha", None),
        P("beta", None, None, None),
        P("beta", None),
        P("alpha", "beta"),
    )
    return jax.shard_map(
        shards, mesh=mesh, in_specs=placed, out_specs=P(None, "alpha", "beta"), check_vma=False
    )
```

profile of v0, /device:TPU:1, one launch (start us, length us, event | category | flops | bytes accessed | tf_op | source)
XLA Modules:
  0.0 348.9 jit_solution(12847920623883171120)
XLA Ops:
  6.5 0.0 copy-start
  6.5 0.0 all-gather.6.cloned.1.call-start
  6.5 0.7 all-gather.6.cloned.1.call-update
  7.3 0.0 all-gather.4.cloned.1.call-start
  7.3 0.7 all-gather.4.cloned.1.call-update
  8.0 2.9 copy.22
  10.9 12.6 %all-to-all-start = ((bf16[8,512,128]{2,0,1:T(8,128)(2,1)}), bf16[8,512,128]{2,0,1:T(8,128)(2,1)}, u32[]{:S(2)}, u32[]{:S(2)}) async-start(bf16[8,512,128]{2,0,1:T(8,128)(2,1)} %copy.22), calls=%async_computation | async-start | bytes 2097152 | tf_op jit(solution)/shard_map/all_to_all | solution.py:21
  23.5 0.7 convert_bitcast_fusion
  24.2 72.8 %all-gather = bf16[32,1,16]{2,1,0:T(2,128)(2,1)S(1)} all-gather(bf16[1,1,16]{2,1,0:T(2,128)(2,1)S(1)} %convert_bitcast_fusion), channel_id=1, replica_groups=mesh['alpha'=8,'beta'=32] {'beta'}, dimensions={0}, use_global_device_ids=true | all-gather | bytes 1056 | tf_op jit(solution)/shard_map/all_gather | solution.py:26
  97.0 0.1 reshape.25
  97.1 0.0 all-to-all-done
  97.1 1.4 copy.23
  98.4 14.9 %gather_fusion.1 = bf16[512,8,16,128]{3,2,1,0:T(8,128)(2,1)} fusion(bf16[8,16,32,128]{3,1,2,0:T(8,128)(2,1)S(1)} %bitcast.62, s32[1024]{0:T(1024)S(1)} %pad_clamp_fusion), kind=kCustom, calls=%fused_computation.1 | custom fusion | bytes 33556480 | tf_op jit(solution)/shard_map/gather | solution.py:29
  113.3 24.0 %all-gather.6.cloned.1.call-done = bf16[32,16,128,128]{3,2,1,0:T(8,128)(2,1)} async-done(((bf16[1,16,128,128]{3,2,1,0:T(8,128)(2,1)}), bf16[32,16,128,128]{3,2,1,0:T(8,128)(2,1)}) %all-gather.6.cloned.1.call-update) | async-done | bytes 16777232 | tf_op jit(solution)/shard_map/all_gather | solution.py:25
  137.3 14.3 %fusion.9 = f32[8,16,32,128]{3,1,0,2:T(8,128)} fusion(bf16[8,16,32,16,128]{4,1,0,3,2:T(8,128)(2,1)} %bitcast.66, bf16[32,16,128,128]{3,2,1,0:T(8,128)(2,1)} %all-gather.6.cloned.1.call-done), kind=kOutput, calls=%fused_computation.10 | convolution fusion | flops 2147483648 | bytes 35651584 | tf_op jit(solution)/shard_map/vtnkj,nkij->vtni/dot_general | solution.py:30
  151.6 9.5 %copy.33 = f32[8,16,32,128]{1,0,3,2:T(8,128)} copy(f32[8,16,32,128]{3,1,0,2:T(8,128)} %fusion.9) | data formatting | bytes 4194304 | tf_op jit(solution)/shard_map/reshape | solution.py:31
  161.1 13.2 %reshape.42 = f32[32,1,16384]{2,1,0:T(1,128)} reshape(f32[4096,8,16]{2,1,0:T(8,128)} %bitcast.64) | data formatting | bytes 4194304
  174.3 20.3 %all-to-all-start.1 = ((f32[32,1,16384]{2,1,0:T(1,128)}), f32[32,1,16384]{2,1,0:T(1,128)}, u32[]{:S(2)}, u32[]{:S(2)}) async-start(f32[32,1,16384]{2,1,0:T(1,128)} %reshape.42), calls=%async_computation.1 | async-start | bytes 4194304 | tf_op jit(solution)/shard_map/all_to_all | solution.py:32
  194.6 0.0 copy-done.3
  194.7 0.1 reshape.17
  194.8 95.1 %all-gather.4.cloned.1.call-done = bf16[8,4096,128]{2,1,0:T(8,128)(2,1)} async-done(((bf16[8,512,128]{2,1,0:T(8,128)(2,1)}), bf16[8,4096,128]{2,1,0:T(8,128)(2,1)}) %all-gather.4.cloned.1.call-update) | async-done | bytes 8388624 | tf_op jit(solution)/shard_map/all_gather | solution.py:11
  289.9 11.0 %gather_fusion = bf16[64,8,128,128]{3,2,1,0:T(8,128)(2,1)} fusion(bf16[8,32,128,128]{3,2,1,0:T(8,128)(2,1)} %bitcast.67, s32[1024]{0:T(1024)S(1)} %pad_clamp_fusion.1), kind=kCustom, calls=%fused_computation | custom fusion | bytes 33554688 | tf_op jit(solution)/shard_map/gather | solution.py:13
  300.9 0.0 copy-done
  300.9 7.1 %fusion.6 = f32[8,4,128,128]{3,2,0,1:T(8,128)S(1)} fusion(bf16[8,4,16,128,128]{4,3,0,2,1:T(8,128)(2,1)} %bitcast.63, bf16[4,16,128,128]{3,2,1,0:T(8,128)(2,1)S(1)} %copy-done), kind=kOutput, calls=%fused_computation.9 | convolution fusion | flops 2147483648 | bytes 20971520 | tf_op jit(solution)/shard_map/rkij,vrkjb->vrib/dot_general | solution.py:14
  307.9 1.5 copy.21
  309.4 0.0 all-to-all-done.1
  309.4 0.5 broadcast.9
  309.9 8.7 %reduce = f32[32,16384]{1,0:T(8,128)} reduce(f32[32,1,16384]{2,1,0:T(1,128)} %all-to-all-done.1, f32[]{:T(128)} %broadcast.9), dimensions={1}, to_apply=%all_to_all.27.reduce_sub_computation | reduce | bytes 4194308 | tf_op jit(solution)/shard_map/all_to_all | solution.py:32
  318.6 9.2 %reshape.43 = f32[4096,8,16]{2,1,0:T(8,128)} reshape(f32[32,16384]{1,0:T(8,128)} %reduce) | data formatting | bytes 4194304
  327.8 10.7 %copy.28 = f32[8,32,16,128]{3,2,1,0:T(8,128)} copy(f32[8,32,16,128]{2,0,3,1:T(8,128)} %bitcast.65) | data formatting | bytes 4194304 | tf_op jit(solution)/shard_map/all_to_all | solution.py:32
  338.5 0.0 copy-done.1
  338.5 3.5 %fusion.5 = bf16[8,512,128]{2,1,0:T(8,128)(2,1)} fusion(f32[8,32,16,128]{3,2,1,0:T(8,128)} %copy.28, f32[8,4,128,128]{3,2,1,0:T(8,128)} %copy.21, bf16[8,512,128]{2,1,0:T(8,128)(2,1)S(1)} %copy-done.1, f32[512,128]{1,0:T(8,128)S(1)} %copy-done.2), kind=kLoop, calls=%fused_computation.8 | loop fusion | flops 2621440 | bytes 6553600 | tf_op jit(solution)/shard_map/convert_element_type | solution.py:39
  (9 shorter events, 0.0 us)
Async XLA Ops:
  6.5 294.3 %copy-start = (bf16[4,16,128,128]{3,2,1,0:T(8,128)(2,1)S(1)}, bf16[4,16,128,128]{3,2,1,0:T(8,128)(2,1)}, u32[]{:S(2)}) copy-start(bf16[4,16,128,128]{3,2,1,0:T(8,128)(2,1)} %param.7) | copy-start | bytes 6291460
  6.5 130.8 %all-gather.6.cloned.1.call-start = ((), (), s32[]{:S(2)}) async-start(), calls=%async_computation.3 | async-start | bytes 17301504 | tf_op jit(solution)/shard_map/all_gather | solution.py:25
  7.3 282.6 %all-gather.4.cloned.1.call-start = ((), (), s32[]{:S(2)}) async-start(), calls=%async_computation.2 | async-start | bytes 9437184 | tf_op jit(solution)/shard_map/all_gather | solution.py:11
  10.9 86.2 %all-to-all-start = ((bf16[8,512,128]{2,0,1:T(8,128)(2,1)}), bf16[8,512,128]{2,0,1:T(8,128)(2,1)}, u32[]{:S(2)}, u32[]{:S(2)}) async-start(bf16[8,512,128]{2,0,1:T(8,128)(2,1)} %copy.22), calls=%async_computation | async-start | bytes 2097152 | tf_op jit(solution)/shard_map/all_to_all | solution.py:21
  161.1 33.5 %copy-start.3 = (s32[4,16]{1,0:T(4,128)S(1)}, s32[4,16]{1,0:T(4,128)}, u32[]{:S(2)}) copy-start(s32[4,16]{1,0:T(4,128)} %param.8) | copy-start | bytes 772
  174.3 135.1 %all-to-all-start.1 = ((f32[32,1,16384]{2,1,0:T(1,128)}), f32[32,1,16384]{2,1,0:T(1,128)}, u32[]{:S(2)}, u32[]{:S(2)}) async-start(f32[32,1,16384]{2,1,0:T(1,128)} %reshape.42), calls=%async_computation.1 | async-start | bytes 4194304 | tf_op jit(solution)/shard_map/all_to_all | solution.py:32
  327.8 10.7 %copy-start.1 = (bf16[8,512,128]{2,1,0:T(8,128)(2,1)S(1)}, bf16[8,512,128]{2,1,0:T(8,128)(2,1)}, u32[]{:S(2)}) copy-start(bf16[8,512,128]{2,1,0:T(8,128)(2,1)} %param.6) | copy-start | bytes 3145732
  327.8 10.7 %copy-start.2 = (f32[512,128]{1,0:T(8,128)S(1)}, f32[512,128]{1,0:T(8,128)}, u32[]{:S(2)}) copy-start(f32[512,128]{1,0:T(8,128)} %param.11) | copy-start | bytes 786436
Sparse Core Ops, SparseCore 0:
  9.9 127.4 all-gather.5
  139.1 150.6 all-gather.3
where the time goes:
time: 350 us; the launch traced here: 349 us
  waiting for transfers between devices  121 us (35%)
  local copies, waits for them, and re-layouts  74.9 us (21%)
  blocking collectives  72.8 us (21%)
  starting transfers between devices  33 us (9%)
  matrix products  21.3 us (6%)
  between operations  13.5 us (4%)
  other arithmetic  13 us (4%)
    all_gather x1, waiting for transfers between devices, alpha_pass(): whole = lax.all_gather(ci_vectors, 'alpha', axis=1, tiled=True)  95.1 us
    all_gather x1, blocking collectives, beta_pass(): lax.all_gather(beta_cols.astype(jnp.bfloat16), 'beta', axis=0, tiled=True)  72.8 us
    unnamed x11, local copies, waits for them, and re-layouts  25.2 us
    all_gather x1, waiting for transfers between devices, beta_pass(): hb_piece = lax.all_gather(beta_blocks, 'beta', axis=0, tiled=True)  24 us
    all_to_all x1, starting transfers between devices, beta_pass(): lax.all_to_all(updated, 'beta', split_axis=2, concat_axis=1, tiled=True)  20.3 us
    gather x1, local copies, waits for them, and re-layouts, beta_pass(): picked = grid[:, :, columns]  14.9 us
    dot_general x1, matrix products, beta_pass(): jnp.einsum('vtnkj,nkij->vtni', picked, hb_piece, preferred_element_type=j...  14.3 us
    all_to_all x1, starting transfers between devices, beta_pass(): lax.all_to_all(ci_vectors, 'beta', split_axis=1, concat_axis=2, tiled=True)  12.6 us
  transfers between devices with their start and end apart: 4, of which 2 were waited for; matrix products, arithmetic and copies ran while one was open for 22% of the time, Pallas kernels for 0%

commit v1 on v0

v1 whole, which is shorter than its diff:
```python
import functools

import jax
import jax.numpy as jnp
from jax import lax
from jax.experimental import pallas as pl
from jax.experimental.pallas import tpu as pltpu
from jax.sharding import PartitionSpec as P

MESH = pl.DeviceIdType.MESH
BF = jnp.bfloat16
F32 = jnp.float32


def kernel(
    c_ref, a_ref, b_ref, ta_ref, tb_ref, d_ref, out_ref,
    ca, cs, co, abuf, bbuf, ia, ib, sa, sb, dg, ad, bd, acc, sig,
    ss, rs, ls,
):
    i = lax.axis_index("alpha")
    j = lax.axis_index("beta")
    l = i // 4
    y = i % 4
    c = j % 2
    x = (j // 2) % 4
    h = j // 8
    z = 2 * h + l

    def dev(xx, yy, zz, cc):
        return ((zz % 2) * 4 + yy, ((zz // 2) * 4 + xx) * 2 + cc)

    def zdev(zz):
        return dev(x, y, zz, c)

    zr = (z + 1) % 8
    zl = (z + 7) % 8
    zin = 2 * h + (1 - l)
    zout = (z + 7 + 2 * l) % 8
    d_xr = dev((x + 1) % 4, y, z, c)
    d_xl = dev((x + 3) % 4, y, z, c)
    d_yr = dev(x, (y + 1) % 4, z, c)
    d_yl = dev(x, (y + 3) % 4, z, c)
    d_co = dev(x, y, z, 1 - c)

    barrier = pltpu.get_barrier_semaphore()
    peers = [zdev((z + d) % 8) for d in range(1, 8)] + [d_xr, d_xl, d_yr, d_yl, d_co]
    for p in peers:
        pl.semaphore_signal(barrier, inc=1, device_id=p, device_id_type=MESH)
    pl.semaphore_wait(barrier, len(peers))

    count = [0]
    sent = []

    def put(src, dst, device):
        k = count[0]
        count[0] += 1
        copy = pltpu.make_async_remote_copy(
            src_ref=src, dst_ref=dst, send_sem=ss.at[k], recv_sem=rs.at[k],
            device_id=device, device_id_type=MESH,
        )
        copy.start()
        sent.append(copy)
        return copy

    lcount = [0]

    def move(src, dst):
        k = lcount[0]
        lcount[0] += 1
        copy = pltpu.make_async_copy(src, dst, ls.at[k])
        copy.start()
        return copy

    own_c = move(c_ref.at[z], ca.at[0, z])
    c_in = []
    for d in (4, 3, 5, 2, 6, 1, 7):
        zz = (z + d) % 8
        c_in.append(put(c_ref.at[zz], ca.at[0, z], zdev(zz)))
    b1 = put(b_ref.at[0], bbuf.at[1, pl.ds(0, 16)], zdev(zout))
    tb1 = put(tb_ref, ib.at[1], zdev(zout))
    a_in = [
        put(a_ref.at[2 * c], abuf.at[4 * l + 2 * c, pl.ds(0, 16)], zdev(zin)),
        put(a_ref.at[2 * c + 1], abuf.at[4 * l + 2 * c + 1, pl.ds(0, 16)], zdev(jnp.where(c == 0, zin, zout))),
    ]
    ta1 = put(ta_ref, ia.at[l], zdev(zin))
    dr = put(d_ref, dg.at[z], zdev(zr))
    dl = put(d_ref, dg.at[z], zdev(zl))
    own = [
        move(a_ref.at[r], abuf.at[4 * l + r, pl.ds(0, 16)]) for r in range(4)
    ] + [
        move(b_ref.at[0], bbuf.at[0, pl.ds(0, 16)]),
        move(ta_ref, ia.at[l]),
        move(tb_ref, ib.at[0]),
        move(d_ref, dg.at[z]),
    ]
    zero = jnp.zeros((128, 128), BF)
    for r in range(8):
        abuf[r, 16] = zero
    for r in range(4):
        bbuf[r, 16] = zero

    own_c.wait()
    for copy in c_in:
        copy.wait_recv()
    mine = ca.at[0]
    yr = put(mine, ca.at[1], d_yr)
    yl = put(mine, ca.at[2], d_yl)
    xr = put(mine, cs.at[0], d_xr)
    xl = put(mine, cs.at[1], d_xl)
    o0 = put(mine, co.at[0], d_co)

    b1.wait_recv()
    b2 = put(bbuf.at[1, pl.ds(0, 16)], bbuf.at[2, pl.ds(0, 16)], zdev(zin))
    tb1.wait_recv()
    tb2 = put(ib.at[1], ib.at[2], zdev(zin))

    def dstep(s, half):
        right = (z + 8 - s) % 8
        left = (z + s) % 8
        if half:
            lo, hi = pl.ds(0, 256), pl.ds(256, 256)
            return (
                put(dg.at[right, lo], dg.at[right, lo], zdev(zr)),
                put(dg.at[left, hi], dg.at[left, hi], zdev(zl)),
            )
        return (
            put(dg.at[right], dg.at[right], zdev(zr)),
            put(dg.at[left], dg.at[left], zdev(zl)),
        )

    dr.wait_recv()
    dl.wait_recv()
    dr, dl = dstep(1, False)
    for copy in a_in:
        copy.wait_recv()
    other = 4 * (1 - l)
    a_x = [
        put(abuf.at[other + 2 * c + k, pl.ds(0, 16)], abuf.at[other + 2 * c + k, pl.ds(0, 16)], d_co)
        for k in range(2)
    ]

    lo, hi = pl.ds(0, 4), pl.ds(4, 4)
    xr.wait_recv()
    xr2 = put(cs.at[0, lo], cs.at[2, lo], d_xr)
    o1 = put(cs.at[0], co.at[1], d_co)
    xl.wait_recv()
    xl2 = put(cs.at[1, hi], cs.at[2, hi], d_xl)
    o2 = put(cs.at[1], co.at[2], d_co)
    yr.wait_recv()
    yr2 = put(ca.at[1, lo], ca.at[3, lo], d_yr)
    yl.wait_recv()
    yl2 = put(ca.at[2, hi], ca.at[3, hi], d_yl)

    b2.wait_recv()
    b3 = put(bbuf.at[2, pl.ds(0, 16)], bbuf.at[3, pl.ds(0, 16)], zdev(zout))
    tb2.wait_recv()
    tb3 = put(ib.at[2], ib.at[3], zdev(zout))
    dr.wait_recv()
    dl.wait_recv()
    dr, dl = dstep(2, False)

    for copy in own:
        copy.wait()
    ta1.wait_recv()
    for copy in a_x:
        copy.wait_recv()
    ta_s = [move(ia, sa)]
    for copy in ta_s:
        copy.wait()

    ys = [y, (y + 3) % 4, (y + 1) % 4, (y + 2) % 4]

    def fill_a(s):
        def body(k, carry):
            col = ((k // 4) * 4 + ys[s]) * 4 + k % 4
            for r in range(8):
                at = sa[r // 4, r % 4, col]
                ad[s, pl.ds(r * 128, 128), pl.ds(pl.multiple_of(k * 128, 128), 128)] = abuf[r, at]
            return carry

        lax.fori_loop(0, 8, body, 0)

    for s in range(4):
        fill_a(s)

    def alpha_dot(s, first):
        def body(m, carry):
            wide = jnp.concatenate(
                [ca[s, pl.ds(2 * q, 2)].reshape(1024, 128) for q in range(4)], axis=1
            )
            lhs = ad[s, pl.ds(pl.multiple_of(m * 256, 256), 256), :]
            res = jnp.dot(lhs, wide, preferred_element_type=F32)
            low = m // 2
            rows = pl.ds(pl.multiple_of((m % 2) * 256, 256), 256)
            for q in range(4):
                piece = res[:, q * 128:(q + 1) * 128]
                if first:
                    acc[2 * q + low, rows, :] = piece
                else:
                    acc[2 * q + low, rows, :] += piece
            return carry

        lax.fori_loop(0, 4, body, 0)

    alpha_dot(0, True)
    alpha_dot(1, False)
    alpha_dot(2, False)

    b3.wait_recv()
    tb3.wait_recv()
    tb_s = move(ib, sb)
    tb_s.wait()
    dr.wait_recv()
    dl.wait_recv()
    dr, dl = dstep(3, True)

    near = (h + 3 + 2 * l) % 4
    far = (h + 1 + 2 * l) % 4
    hs = [h, near, far, (h + 2) % 4]
    xs = [x, (x + 3) % 4, (x + 1) % 4, (x + 2) % 4]

    def fill_b(s):
        cc = c if s < 4 else 1 - c
        xx = xs[s % 4]

        def body(k, carry):
            col = (k * 4 + xx) * 2 + cc
            for r in range(4):
                at = sb[r, 0, col]
                rows = pl.ds(pl.multiple_of(hs[r] * 128, 128), 128)
                bd[s, rows, pl.ds(pl.multiple_of(k * 128, 128), 128)] = bbuf[r, at]
            return carry

        lax.fori_loop(0, 4, body, 0)

    for s in range(8):
        fill_b(s)

    def beta_dot(s):
        if s == 0:
            src = ca.at[0]
        elif s < 4:
            src = cs.at[s - 1]
        else:
            src = co.at[s - 4]

        def body(m, carry):
            low = m // 2
            rows = pl.ds(pl.multiple_of((m % 2) * 256, 256), 256)
            lhs = jnp.concatenate([src[2 * q + low, rows, :] for q in range(4)], axis=1)
            res = lax.dot_general(lhs, bd[s], (((1,), (1,)), ((), ())), preferred_element_type=F32)
            for q in range(4):
                acc[2 * q + low, rows, :] += res[:, q * 128:(q + 1) * 128]
            return carry

        lax.fori_loop(0, 4, body, 0)

    beta_dot(0)
    beta_dot(1)
    beta_dot(2)
    o0.wait_recv()
    beta_dot(4)
    o1.wait_recv()
    beta_dot(5)
    o2.wait_recv()
    beta_dot(6)
    xr2.wait_recv()
    xl2.wait_recv()
    o3 = put(cs.at[2], co.at[3], d_co)
    beta_dot(3)
    yr2.wait_recv()
    yl2.wait_recv()
    alpha_dot(3, False)
    o3.wait_recv()
    beta_dot(7)
    dr.wait_recv()
    dl.wait_recv()

    outs = []
    for d in (4, 3, 5, 2, 6, 1, 7, 0):
        zz = (z + d) % 8
        sig[zz] = (acc[zz] + dg[zz] * ca[0, zz].astype(F32)).astype(BF)
        if d:
            outs.append(put(sig.at[zz], out_ref.at[z], zdev(zz)))
        else:
            last = move(sig.at[zz], out_ref.at[zz])
    last.wait()
    for copy in outs:
        copy.wait_recv()
    for copy in sent:
        copy.wait_send()


def slots(cols):
    hit = cols[:, None, :] == jnp.arange(32, dtype=jnp.int32)[None, :, None]
    order = jnp.arange(16, dtype=jnp.int32)
    table = jnp.min(jnp.where(hit, order, 16), axis=-1).astype(jnp.int32)
    return jnp.pad(table, ((0, 8 - table.shape[0]), (0, 96)))


def shards(ci_vectors, alpha_blocks, alpha_cols, beta_blocks, beta_cols, diagonal):
    anywhere = pl.BlockSpec(memory_space=pl.ANY)
    hbm = pl.BlockSpec(memory_space=pltpu.MemorySpace.HBM)
    return pl.pallas_call(
        kernel,
        out_shape=jax.ShapeDtypeStruct((8, 512, 128), BF),
        in_specs=[hbm] * 6,
        out_specs=hbm,
        scratch_shapes=[
            pltpu.VMEM((4, 8, 512, 128), BF),
            pltpu.VMEM((3, 8, 512, 128), BF),
            pltpu.VMEM((4, 8, 512, 128), BF),
            pltpu.VMEM((8, 17, 128, 128), BF),
            pltpu.VMEM((4, 17, 128, 128), BF),
            pltpu.VMEM((2, 8, 128), jnp.int32),
            pltpu.VMEM((4, 8, 128), jnp.int32),
            pltpu.SMEM((2, 8, 128), jnp.int32),
            pltpu.SMEM((4, 8, 128), jnp.int32),
            pltpu.VMEM((8, 512, 128), F32),
            pltpu.VMEM((4, 1024, 1024), BF),
            pltpu.VMEM((8, 512, 512), BF),
            pltpu.VMEM((8, 512, 128), F32),
            pltpu.VMEM((8, 512, 128), BF),
            pltpu.SemaphoreType.DMA((64,)),
            pltpu.SemaphoreType.DMA((64,)),
            pltpu.SemaphoreType.DMA((16,)),
        ],
        compiler_params=pltpu.CompilerParams(
            collective_id=0, has_side_effects=True, vmem_limit_bytes=60 * 1024 * 1024
        ),
    )(ci_vectors, alpha_blocks, beta_blocks, slots(alpha_cols), slots(beta_cols), diagonal)


def solution(mesh):
    placed = (
        P(None, "alpha", "beta"),
        P("alpha", None, None, None),
        P("alpha", None),
        P("beta", None, None, None),
        P("beta", None),
        P("alpha", "beta"),
    )
    return jax.shard_map(
        shards, mesh=mesh, in_specs=placed, out_specs=P(None, "alpha", "beta"), check_vma=False
    )
```

time: 350 us -> 128 us (0.37)
  Pallas kernels: 0 us -> 123 us
  waiting for transfers between devices: 121 us -> 0 us
  blocking collectives: 72.8 us -> 0 us
  local copies, waits for them, and re-layouts: 74.9 us -> 3.46 us
  starting transfers between devices: 33 us -> 0 us
  matrix products: 21.3 us -> 0 us
  between operations: 13.5 us -> 0.01 us
  other arithmetic: 13 us -> 1.51 us
    pallas_call x0 -> x1, Pallas kernels: none -> 123 us  [shards(): pl.pallas_call(kernel, out_shape=jax.ShapeDtypeStruct((8, 512, 128), BF),...]
    all_gather x2 -> x0, waiting for transfers between devices: 119 us -> none  [the longest x1 95.1 us: alpha_pass(): whole = lax.all_gather(ci_vectors, 'alpha', axis=1, tiled=True)]
    all_gather x1 -> x0, blocking collectives: 72.8 us -> none  [beta_pass(): lax.all_gather(beta_cols.astype(jnp.bfloat16), 'beta', axis=0, tiled=True)]
    all_to_all x2 -> x0, starting transfers between devices: 33 us -> none  [the longest x1 20.3 us: beta_pass(): lax.all_to_all(updated, 'beta', split_axis=2, concat_axis=1, tiled=True)]
    gather x2 -> x0, local copies, waits for them, and re-layouts: 25.9 us -> none  [the longest x1 14.9 us: beta_pass(): picked = grid[:, :, columns]]
    unnamed x11 -> x1, local copies, waits for them, and re-layouts: 25.2 us -> 2.27 us
    dot_general x2 -> x0, matrix products: 21.3 us -> none  [the longest x1 14.3 us: beta_pass(): jnp.einsum('vtnkj,nkij->vtni', picked, hb_piece, preferred_element_type=j...]
    all_to_all x3 -> x0, local copies, waits for them, and re-layouts: 12.6 us -> none  [the longest x2 11.2 us: beta_pass(): lax.all_to_all(updated, 'beta', split_axis=2, concat_axis=1, tiled=True)]
  transfers between devices with their start and end apart: 4 -> 0, of which waited for: 2 -> 0; matrix products, arithmetic and copies ran while one was open for 22% -> 0% of each run, Pallas kernels for 0% -> 0%
where the time goes in v1:
time: 128 us
  Pallas kernels  123 us (96%)
  local copies, waits for them, and re-layouts  3.46 us (3%)
  other arithmetic  1.51 us (1%)
    pallas_call x1, Pallas kernels, shards(): pl.pallas_call(kernel, out_shape=jax.ShapeDtypeStruct((8, 512, 128), BF),...  123 us

profile of v1, /device:TPU:1, one launch (start us, length us, event | category | flops | bytes accessed | tf_op | source)
XLA Modules:
  0.0 128.3 jit_solution(2245695007676109163)
XLA Ops:
  0.0 0.7 select_reduce_fusion.1
  0.7 0.8 select_reduce_fusion
  1.5 0.6 pad.8.ta_ref
  2.1 0.6 pad.9.tb_ref
  2.7 123.3 %shard_map.64 = bf16[8,512,128]{2,1,0:T(8,128)(2,1)} custom-call(bf16[8,512,128]{2,1,0:T(8,128)(2,1)} %c_ref.1, bf16[4,16,128,128]{3,2,1,0:T(8,128)(2,1)} %a_ref.1, bf16[1,16,128,128]{3,2,1,0:T(8,128)(2,1)} %b_ref.1, s32[8,128]{1,0:T(8,128)} %pad.8.ta_ref, s32[8,128]{1,0:T(8,128)} %pad.9.tb_ref, f32[512,128]{1,0:T(8,128)} %d_ref.1), custom_call_target="tpu_custom_call" | custom-call | tf_op jit(solution)/shard_map/pallas_call | solution.py:304
  126.0 2.3 %copy.8 = bf16[8,512,128]{2,1,0:T(8,128)(2,1)} copy(bf16[8,512,128]{2,1,0:T(8,128)(2,1)} %shard_map.64) | data formatting | bytes 2097152

commit v2 on v1

v2 whole, which is shorter than its diff:
```python
import jax
import jax.numpy as jnp
from jax import lax
from jax.experimental import pallas as pl
from jax.experimental.pallas import tpu as pltpu
from jax.sharding import PartitionSpec as P

MESH = pl.DeviceIdType.MESH
BF = jnp.bfloat16
F32 = jnp.float32


def kernel(
    c_ref, a_ref, b_ref, t_ref, d_ref, out_ref,
    ca, cs, co, abuf, bbuf, ia, ib, sa, sb, dg, ad, bd, acc, sig,
    ss, rs, ls,
):
    i = lax.axis_index("alpha")
    j = lax.axis_index("beta")
    l = i // 4
    y = i % 4
    c = j % 2
    x = (j // 2) % 4
    h = j // 8
    z = 2 * h + l

    def dev(xx, yy, zz, cc):
        return ((zz % 2) * 4 + yy, ((zz // 2) * 4 + xx) * 2 + cc)

    def zdev(zz):
        return dev(x, y, zz, c)

    zr = (z + 1) % 8
    zl = (z + 7) % 8
    zin = 2 * h + (1 - l)
    zout = (z + 7 + 2 * l) % 8
    d_xr = dev((x + 1) % 4, y, z, c)
    d_xl = dev((x + 3) % 4, y, z, c)
    d_yr = dev(x, (y + 1) % 4, z, c)
    d_yl = dev(x, (y + 3) % 4, z, c)
    d_co = dev(x, y, z, 1 - c)

    barrier = pltpu.get_barrier_semaphore()
    peers = [zdev((z + d) % 8) for d in range(1, 8)] + [d_xr, d_xl, d_yr, d_yl, d_co]
    for p in peers:
        pl.semaphore_signal(barrier, inc=1, device_id=p, device_id_type=MESH)
    pl.semaphore_wait(barrier, len(peers))

    count = [0]
    sent = []

    def put(src, dst, device):
        k = count[0]
        count[0] += 1
        copy = pltpu.make_async_remote_copy(
            src_ref=src, dst_ref=dst, send_sem=ss.at[k], recv_sem=rs.at[k],
            device_id=device, device_id_type=MESH,
        )
        copy.start()
        sent.append(copy)
        return copy

    lcount = [0]

    def move(src, dst):
        k = lcount[0]
        lcount[0] += 1
        copy = pltpu.make_async_copy(src, dst, ls.at[k])
        copy.start()
        return copy

    cuts = ((0, 128), (128, 128), (256, 256))
    chunk = [pl.ds(a, n) for a, n in cuts]
    own_c = move(c_ref.at[z], ca.at[0, z])
    c_in = ([], [], [])

    def turn(k):
        for d in (4, 3, 5, 2, 6, 1, 7):
            zz = (z + d) % 8
            c_in[k].append(put(c_ref.at[zz, chunk[k]], ca.at[0, z, chunk[k]], zdev(zz)))

    quarter = pl.ds(4 * y, 4)
    part = pl.ds(8 * c, 8)
    b1 = put(b_ref.at[0, quarter], bbuf.at[1, quarter], zdev(zout))
    tb_in = [put(t_ref, ib.at[d], zdev((z + 8 + (2 * l - 1) * d) % 8)) for d in (3, 2, 1)]
    ta_in = put(t_ref, ia.at[l], zdev(zin))
    turn(0)
    a_in = put(a_ref.at[x, part], abuf.at[4 * l + x, part], zdev(jnp.where(c == 0, zin, zout)))
    own = [
        move(a_ref.at[r], abuf.at[4 * l + r, pl.ds(0, 16)]) for r in range(4)
    ] + [
        move(b_ref.at[0], bbuf.at[0, pl.ds(0, 16)]),
        move(t_ref, ia.at[l]),
        move(t_ref, ib.at[0]),
        move(d_ref, dg.at[z]),
    ]
    zero = jnp.zeros((128, 128), BF)
    for r in range(8):
        abuf[r, 16] = zero
    for r in range(4):
        bbuf[r, 16] = zero

    full, lo, hi = pl.ds(0, 8), pl.ds(0, 4), pl.ds(4, 4)

    def spread(k):
        for copy in c_in[k]:
            copy.wait_recv()
        mine = ca.at[0, full, chunk[k]]
        return (
            put(mine, ca.at[1, full, chunk[k]], d_yr),
            put(mine, cs.at[0, full, chunk[k]], d_xr),
            put(mine, ca.at[2, full, chunk[k]], d_yl),
            put(mine, cs.at[1, full, chunk[k]], d_xl),
            put(mine, co.at[0, full, chunk[k]], d_co),
        )

    def across_x(k, first):
        _, xr, _, xl, _ = first
        xr.wait_recv()
        xr2 = put(cs.at[0, lo, chunk[k]], cs.at[2, lo, chunk[k]], d_xr)
        xl.wait_recv()
        xl2 = put(cs.at[1, hi, chunk[k]], cs.at[2, hi, chunk[k]], d_xl)
        o = put(cs.at[pl.ds(0, 2), full, chunk[k]], co.at[pl.ds(1, 2), full, chunk[k]], d_co)
        return xr2, xl2, o

    def across_y(k, first):
        yr, _, yl, _, _ = first
        yr.wait_recv()
        yr2 = put(ca.at[1, lo, chunk[k]], ca.at[3, lo, chunk[k]], d_yr)
        yl.wait_recv()
        yl2 = put(ca.at[2, hi, chunk[k]], ca.at[3, hi, chunk[k]], d_yl)
        return yr2, yl2

    def last_core(k, second):
        second[0].wait_recv()
        second[1].wait_recv()
        return put(cs.at[2, full, chunk[k]], co.at[3, full, chunk[k]], d_co)

    def dstep(s, half):
        right = (z + 8 - s) % 8
        left = (z + s) % 8
        if half:
            rlo, rhi = pl.ds(0, 256), pl.ds(256, 256)
            return (
                put(dg.at[right, rlo], dg.at[right, rlo], zdev(zr)),
                put(dg.at[left, rhi], dg.at[left, rhi], zdev(zl)),
            )
        return (
            put(dg.at[right], dg.at[right], zdev(zr)),
            put(dg.at[left], dg.at[left], zdev(zl)),
        )

    b1.wait_recv()
    b2 = put(bbuf.at[1, quarter], bbuf.at[2, quarter], zdev(zin))
    turn(1)
    own_c.wait()
    f0 = spread(0)
    b2.wait_recv()
    b3 = put(bbuf.at[2, quarter], bbuf.at[3, quarter], zdev(zout))
    turn(2)
    dr = put(d_ref, dg.at[z], zdev(zr))
    dl = put(d_ref, dg.at[z], zdev(zl))
    other = 4 * (1 - l)
    a_in.wait_recv()
    piece = abuf.at[other + x, part]
    axr = put(piece, piece, d_xr)
    axl = put(piece, piece, d_xl)
    n0 = across_x(0, f0)
    m0 = across_y(0, f0)
    f1 = spread(1)
    b3.wait_recv()
    three = pl.ds(1, 3)
    piece = bbuf.at[three, quarter]
    byr = put(piece, piece, d_yr)
    byl = put(piece, piece, d_yl)
    axr.wait_recv()
    piece = abuf.at[other + (x + 3) % 4, pl.ds(8 * c, 4)]
    axr2 = put(piece, piece, d_xr)
    axl.wait_recv()
    piece = abuf.at[other + (x + 1) % 4, pl.ds(8 * c + 4, 4)]
    axl2 = put(piece, piece, d_xl)
    o0 = last_core(0, n0)
    n1 = across_x(1, f1)
    m1 = across_y(1, f1)
    axr2.wait_recv()
    axl2.wait_recv()
    piece = abuf.at[pl.ds(other, 4), part]
    a_x = put(piece, piece, d_co)

    for copy in own:
        copy.wait()
    ta_in.wait_recv()
    for copy in tb_in:
        copy.wait_recv()
    ta_s = move(ia, sa)
    tb_s = move(ib, sb)
    ta_s.wait()
    tb_s.wait()
    o1 = last_core(1, n1)
    a_x.wait_recv()
    ys = [y, (y + 3) % 4, (y + 1) % 4, (y + 2) % 4]

    def fill_a(s):
        def body(t, carry):
            col = ((t // 2 % 2) * 4 + ys[s]) * 4 + (t // 4) * 2 + t % 2
            for r in range(8):
                at = sa[r // 4, r % 4, col]
                ad[s, pl.ds(r * 128, 128), pl.ds(pl.multiple_of(t * 128, 128), 128)] = abuf[r, at]
            return carry

        lax.fori_loop(0, 8, body, 0)

    for s in range(4):
        fill_a(s)

    half = (pl.ds(0, 256), pl.ds(256, 256))

    def alpha_dot(s, k, fresh=False):
        wide = jnp.concatenate(
            [ca[s, pl.ds(2 * q, 2), half[k]].reshape(512, 128) for q in range(4)], axis=1
        )
        res = jnp.dot(ad[s, :, pl.ds(512 * k, 512)], wide, preferred_element_type=F32)
        for q in range(4):
            piece = res[:, q * 128:(q + 1) * 128].reshape(2, 512, 128)
            if fresh:
                acc[pl.ds(2 * q, 2)] = piece
            else:
                acc[pl.ds(2 * q, 2)] += piece

    near = (h + 3 + 2 * l) % 4
    far = (h + 1 + 2 * l) % 4
    hs = [h, near, far, (h + 2) % 4]
    xs = [x, (x + 3) % 4, (x + 1) % 4, (x + 2) % 4]

    def fill_b(s):
        cc = c if s < 4 else 1 - c
        xx = xs[s % 4]

        def body(t, carry):
            col = (t * 4 + xx) * 2 + cc
            for r in range(4):
                at = sb[r, 4, col]
                rows = pl.ds(pl.multiple_of(hs[r] * 128, 128), 128)
                bd[s, rows, pl.ds(pl.multiple_of(t * 128, 128), 128)] = bbuf[r, at]
            return carry

        lax.fori_loop(0, 4, body, 0)

    def beta_dot(s, k):
        if s == 0:
            src = ca.at[0]
        elif s < 4:
            src = cs.at[s - 1]
        else:
            src = co.at[s - 4]

        lhs = jnp.concatenate(
            [src[pl.ds(2 * q, 2), half[k], :].reshape(512, 128) for q in range(4)], axis=1
        )
        res = lax.dot_general(lhs, bd[s], (((1,), (1,)), ((), ())), preferred_element_type=F32)
        for q in range(4):
            acc[pl.ds(2 * q, 2), half[k], :] += res[:, q * 128:(q + 1) * 128].reshape(2, 256, 128)

    byr.wait_recv()
    piece = bbuf.at[three, pl.ds(4 * ((y + 3) % 4), 2)]
    byr2 = put(piece, piece, d_yr)
    byl.wait_recv()
    piece = bbuf.at[three, pl.ds(4 * ((y + 1) % 4) + 2, 2)]
    byl2 = put(piece, piece, d_yl)
    f2 = spread(2)
    alpha_dot(0, 0, True)
    alpha_dot(1, 0)
    alpha_dot(2, 0)
    for copy in m0 + m1:
        copy.wait_recv()
    alpha_dot(3, 0)
    dr.wait_recv()
    dl.wait_recv()
    dr, dl = dstep(1, False)
    byr2.wait_recv()
    byl2.wait_recv()
    for s in range(8):
        fill_b(s)
    for s in range(4):
        beta_dot(s, 0)
    f0[4].wait_recv()
    f1[4].wait_recv()
    dr.wait_recv()
    dl.wait_recv()
    dr, dl = dstep(2, False)
    beta_dot(4, 0)
    n0[2].wait_recv()
    n1[2].wait_recv()
    beta_dot(5, 0)
    beta_dot(6, 0)
    n2 = across_x(2, f2)
    o0.wait_recv()
    o1.wait_recv()
    beta_dot(7, 0)
    alpha_dot(0, 1)
    beta_dot(0, 1)
    dr.wait_recv()
    dl.wait_recv()
    dr, dl = dstep(3, True)
    m2 = across_y(2, f2)
    beta_dot(1, 1)
    beta_dot(2, 1)
    o2 = last_core(2, n2)
    f2[4].wait_recv()
    beta_dot(4, 1)
    n2[2].wait_recv()
    beta_dot(5, 1)
    beta_dot(6, 1)
    beta_dot(3, 1)
    alpha_dot(1, 1)
    alpha_dot(2, 1)
    o2.wait_recv()
    beta_dot(7, 1)
    for copy in m2:
        copy.wait_recv()
    alpha_dot(3, 1)
    dr.wait_recv()
    dl.wait_recv()

    outs = []
    for d in (4, 3, 5, 2, 6, 1, 7, 0):
        zz = (z + d) % 8

        def finish(t, carry):
            rows = pl.ds(pl.multiple_of(t * 128, 128), 128)
            whole = acc[zz, rows] + dg[zz, rows] * ca[0, zz, rows].astype(F32)
            sig[zz, rows] = whole.astype(BF)
            return carry

        lax.fori_loop(0, 4, finish, 0)
        if d:
            outs.append(put(sig.at[zz], out_ref.at[z], zdev(zz)))
        else:
            last = move(sig.at[zz], out_ref.at[zz])
    last.wait()
    for copy in outs:
        copy.wait_recv()
    for copy in sent:
        copy.wait_send()


def slots(alpha_cols, beta_cols):
    rows = jnp.arange(8)[:, None, None]
    a = jnp.pad(alpha_cols, ((0, 4), (0, 0)))[:, None, :]
    cols = jnp.where(rows == 4, beta_cols[None], a)
    hit = cols == jnp.arange(128, dtype=jnp.int32)[None, :, None]
    return jnp.min(jnp.where(hit, jnp.arange(16, dtype=jnp.int32), 16), axis=-1)


def shards(ci_vectors, alpha_blocks, alpha_cols, beta_blocks, beta_cols, diagonal):
    hbm = pl.BlockSpec(memory_space=pltpu.MemorySpace.HBM)
    return pl.pallas_call(
        kernel,
        out_shape=jax.ShapeDtypeStruct((8, 512, 128), BF),
        in_specs=[hbm] * 5,
        out_specs=hbm,
        scratch_shapes=[
            pltpu.VMEM((4, 8, 512, 128), BF),
            pltpu.VMEM((3, 8, 512, 128), BF),
            pltpu.VMEM((4, 8, 512, 128), BF),
            pltpu.VMEM((8, 17, 128, 128), BF),
            pltpu.VMEM((4, 17, 128, 128), BF),
            pltpu.VMEM((2, 8, 128), jnp.int32),
            pltpu.VMEM((4, 8, 128), jnp.int32),
            pltpu.SMEM((2, 8, 128), jnp.int32),
            pltpu.SMEM((4, 8, 128), jnp.int32),
            pltpu.VMEM((8, 512, 128), F32),
            pltpu.VMEM((4, 1024, 1024), BF),
            pltpu.VMEM((8, 512, 512), BF),
            pltpu.VMEM((8, 512, 128), F32),
            pltpu.VMEM((8, 512, 128), BF),
            pltpu.SemaphoreType.DMA((112,)),
            pltpu.SemaphoreType.DMA((112,)),
            pltpu.SemaphoreType.DMA((16,)),
        ],
        compiler_params=pltpu.CompilerParams(
            collective_id=0, has_side_effects=True, vmem_limit_bytes=60 * 1024 * 1024
        ),
    )(ci_vectors, alpha_blocks, beta_blocks, slots(alpha_cols, beta_cols), diagonal)


def solution(mesh):
    placed = (
        P(None, "alpha", "beta"),
        P("alpha", None, None, None),
        P("alpha", None),
        P("beta", None, None, None),
        P("beta", None),
        P("alpha", "beta"),
    )
    return jax.shard_map(
        shards, mesh=mesh, in_specs=placed, out_specs=P(None, "alpha", "beta"), check_vma=False
    )
```

time: 128 us -> 108 us (0.84)
  Pallas kernels: 123 us -> 104 us
    pallas_call x1, Pallas kernels: 123 us -> 104 us  [shards(): pl.pallas_call(kernel, out_shape=jax.ShapeDtypeStruct((8, 512, 128), BF),...]
where the time goes in v2:
time: 108 us; the launch traced here: 107 us
  Pallas kernels  104 us (96%)
  local copies, waits for them, and re-layouts  2.27 us (2%)
  other arithmetic  1.45 us (1%)
    pallas_call x1, Pallas kernels, shards(): pl.pallas_call(kernel, out_shape=jax.ShapeDtypeStruct((8, 512, 128), BF),...  104 us
    unnamed x1, local copies, waits for them, and re-layouts  2.27 us

profile of v2, /device:TPU:1, one launch (start us, length us, event | category | flops | bytes accessed | tf_op | source)
XLA Modules:
  0.0 107.5 jit_solution(11464993499594656904)
XLA Ops:
  0.0 0.8 pad_select_fusion
  0.8 0.7 select_reduce_fusion.t_ref
  1.5 103.7 %shard_map.64 = bf16[8,512,128]{2,1,0:T(8,128)(2,1)} custom-call(bf16[8,512,128]{2,1,0:T(8,128)(2,1)} %c_ref.1, bf16[4,16,128,128]{3,2,1,0:T(8,128)(2,1)} %a_ref.1, bf16[1,16,128,128]{3,2,1,0:T(8,128)(2,1)} %b_ref.1, s32[8,128]{1,0:T(8,128)} %select_reduce_fusion.t_ref, f32[512,128]{1,0:T(8,128)} %d_ref.1), custom_call_target="tpu_custom_call" | custom-call | tf_op jit(solution)/shard_map/pallas_call | solution.py:357
  105.2 2.3 %copy.8 = bf16[8,512,128]{2,1,0:T(8,128)(2,1)} copy(bf16[8,512,128]{2,1,0:T(8,128)(2,1)} %shard_map.64) | data formatting | bytes 2097152
  (1 shorter events, 0.0 us)

commit v3 on v2

--- a/solution.py
+++ b/solution.py
@@ -11,8 +11,8 @@
 
 
 def kernel(
-    c_ref, a_ref, b_ref, t_ref, d_ref, out_ref,
-    ca, cs, co, abuf, bbuf, ia, ib, sa, sb, dg, ad, bd, acc, sig,
+    c_ref, a_ref, ac_ref, b_ref, bc_ref, d_ref, out_ref,
+    ca, cs, co, abuf, bbuf, tab, ia, ib, sac, sbc, sa, sb, dg, ad, bd, acc, sig,
     ss, rs, ls,
 ):
     i = lax.axis_index("alpha")
@@ -69,10 +69,11 @@
         copy.start()
         return copy
 
-    cuts = ((0, 128), (128, 128), (256, 256))
-    chunk = [pl.ds(a, n) for a, n in cuts]
+    cols_in = [move(ac_ref, sac), move(bc_ref, sbc)]
+    chunk = [pl.ds(128 * k, 128) for k in range(4)]
+    half = (pl.ds(0, 256), pl.ds(256, 256))
     own_c = move(c_ref.at[z], ca.at[0, z])
-    c_in = ([], [], [])
+    c_in = ([], [], [], [])
 
     def turn(k):
         for d in (4, 3, 5, 2, 6, 1, 7):
@@ -81,17 +82,14 @@
 
     quarter = pl.ds(4 * y, 4)
     part = pl.ds(8 * c, 8)
+    turn(0)
     b1 = put(b_ref.at[0, quarter], bbuf.at[1, quarter], zdev(zout))
-    tb_in = [put(t_ref, ib.at[d], zdev((z + 8 + (2 * l - 1) * d) % 8)) for d in (3, 2, 1)]
-    ta_in = put(t_ref, ia.at[l], zdev(zin))
-    turn(0)
+    turn(1)
     a_in = put(a_ref.at[x, part], abuf.at[4 * l + x, part], zdev(jnp.where(c == 0, zin, zout)))
     own = [
         move(a_ref.at[r], abuf.at[4 * l + r, pl.ds(0, 16)]) for r in range(4)
     ] + [
         move(b_ref.at[0], bbuf.at[0, pl.ds(0, 16)]),
-        move(t_ref, ia.at[l]),
-        move(t_ref, ib.at[0]),
         move(d_ref, dg.at[z]),
     ]
     zero = jnp.zeros((128, 128), BF)
@@ -100,6 +98,15 @@
     for r in range(4):
         bbuf[r, 16] = zero
 
+    cols_in[0].wait()
+    cols_in[1].wait()
+    lane = lax.broadcasted_iota(jnp.int32, (1, 128), 1)
+    for r in range(5):
+        line = jnp.full((1, 128), 16, jnp.int32)
+        for k in range(16):
+            line = jnp.where(lane == (sac[r, k] if r < 4 else sbc[0, k]), k, line)
+        tab[pl.ds(r, 1), :] = line
+
     full, lo, hi = pl.ds(0, 8), pl.ds(0, 4), pl.ds(4, 4)
 
     def spread(k):
@@ -107,12 +114,30 @@
             copy.wait_recv()
         mine = ca.at[0, full, chunk[k]]
         return (
-            put(mine, ca.at[1, full, chunk[k]], d_yr),
+            put(mine, ca.at[1, full, chunk[k]], d_yr) if k < 2 else None,
             put(mine, cs.at[0, full, chunk[k]], d_xr),
-            put(mine, ca.at[2, full, chunk[k]], d_yl),
+            put(mine, ca.at[2, full, chunk[k]], d_yl) if k < 2 else None,
             put(mine, cs.at[1, full, chunk[k]], d_xl),
             put(mine, co.at[0, full, chunk[k]], d_co),
         )
+
+    def cols(g, k):
+        return pl.ds(4 * k + 2 * ((h + 1 - g) % 2), 2)
+
+    def group_y(g, k):
+        src = ca.at[0, cols(g, k), half[1]]
+        return (
+            put(src, ca.at[1, cols(g, k), half[1]], d_yr),
+            put(src, ca.at[2, cols(g, k), half[1]], d_yl),
+        )
+
+    def group_right(g, pair):
+        pair[0].wait_recv()
+        return put(ca.at[1, cols(g, 0), half[1]], ca.at[3, cols(g, 0), half[1]], d_yr)
+
+    def group_left(g, pair):
+        pair[1].wait_recv()
+        return put(ca.at[2, cols(g, 1), half[1]], ca.at[3, cols(g, 1), half[1]], d_yl)
 
     def across_x(k, first):
         _, xr, _, xl, _ = first
@@ -150,42 +175,56 @@
             put(dg.at[left], dg.at[left], zdev(zl)),
         )
 
+    own_c.wait()
+    f0 = spread(0)
+    tb_in = [put(tab, ib.at[d], zdev((z + 8 + (2 * l - 1) * d) % 8)) for d in (3, 2, 1)]
+    ta_in = put(tab, ia.at[l], zdev(zin))
+    own += [move(tab, ia.at[l]), move(tab, ib.at[0])]
     b1.wait_recv()
     b2 = put(bbuf.at[1, quarter], bbuf.at[2, quarter], zdev(zin))
-    turn(1)
-    own_c.wait()
-    f0 = spread(0)
-    b2.wait_recv()
-    b3 = put(bbuf.at[2, quarter], bbuf.at[3, quarter], zdev(zout))
-    turn(2)
-    dr = put(d_ref, dg.at[z], zdev(zr))
-    dl = put(d_ref, dg.at[z], zdev(zl))
+    n0 = across_x(0, f0)
+    m0 = across_y(0, f0)
+    f1 = spread(1)
     other = 4 * (1 - l)
     a_in.wait_recv()
     piece = abuf.at[other + x, part]
     axr = put(piece, piece, d_xr)
     axl = put(piece, piece, d_xl)
-    n0 = across_x(0, f0)
-    m0 = across_y(0, f0)
-    f1 = spread(1)
+    b2.wait_recv()
+    b3 = put(bbuf.at[2, quarter], bbuf.at[3, quarter], zdev(zout))
+    dr = put(d_ref, dg.at[z], zdev(zr))
+    dl = put(d_ref, dg.at[z], zdev(zl))
+    turn(2)
+    turn(3)
+    o0 = last_core(0, n0)
     b3.wait_recv()
     three = pl.ds(1, 3)
     piece = bbuf.at[three, quarter]
     byr = put(piece, piece, d_yr)
     byl = put(piece, piece, d_yl)
+    n1 = across_x(1, f1)
+    m1 = across_y(1, f1)
+    dr.wait_recv()
+    dl.wait_recv()
+    dr, dl = dstep(1, False)
     axr.wait_recv()
     piece = abuf.at[other + (x + 3) % 4, pl.ds(8 * c, 4)]
     axr2 = put(piece, piece, d_xr)
     axl.wait_recv()
     piece = abuf.at[other + (x + 1) % 4, pl.ds(8 * c + 4, 4)]
     axl2 = put(piece, piece, d_xl)
-    o0 = last_core(0, n0)
-    n1 = across_x(1, f1)
-    m1 = across_y(1, f1)
+    o1 = last_core(1, n1)
+    f2 = spread(2)
     axr2.wait_recv()
     axl2.wait_recv()
     piece = abuf.at[pl.ds(other, 4), part]
     a_x = put(piece, piece, d_co)
+    byr.wait_recv()
+    piece = bbuf.at[three, pl.ds(4 * ((y + 3) % 4), 2)]
+    byr2 = put(piece, piece, d_yr)
+    byl.wait_recv()
+    piece = bbuf.at[three, pl.ds(4 * ((y + 1) % 4) + 2, 2)]
+    byl2 = put(piece, piece, d_yl)
 
     for copy in own:
         copy.wait()
@@ -196,7 +235,6 @@
     tb_s = move(ib, sb)
     ta_s.wait()
     tb_s.wait()
-    o1 = last_core(1, n1)
     a_x.wait_recv()
     ys = [y, (y + 3) % 4, (y + 1) % 4, (y + 2) % 4]
 
@@ -213,8 +251,6 @@
     for s in range(4):
         fill_a(s)
 
-    half = (pl.ds(0, 256), pl.ds(256, 256))
-
     def alpha_dot(s, k, fresh=False):
         wide = jnp.concatenate(
             [ca[s, pl.ds(2 * q, 2), half[k]].reshape(512, 128) for q in range(4)], axis=1
@@ -227,6 +263,14 @@
             else:
                 acc[pl.ds(2 * q, 2)] += piece
 
+    def alpha_group(s, g):
+        wide = jnp.concatenate(
+            [ca[s, cols(g, q), half[1]].reshape(512, 128) for q in range(2)], axis=1
+        )
+        res = jnp.dot(ad[s, :, pl.ds(512, 512)], wide, preferred_element_type=F32)
+        for q in range(2):
+            acc[cols(g, q)] += res[:, q * 128:(q + 1) * 128].reshape(2, 512, 128)
+
     near = (h + 3 + 2 * l) % 4
     far = (h + 1 + 2 * l) % 4
     hs = [h, near, far, (h + 2) % 4]
@@ -246,86 +290,89 @@
 
         lax.fori_loop(0, 4, body, 0)
 
-    def beta_dot(s, k):
+    def beta_source(s):
         if s == 0:
-            src = ca.at[0]
-        elif s < 4:
-            src = cs.at[s - 1]
+            return ca.at[0]
+        return cs.at[s - 1] if s < 4 else co.at[s - 4]
+
+    def beta_dot(some, k, g=None):
+        lhs = jnp.concatenate(
+            [beta_source(s)[pl.ds(2 * q, 2), half[k], :].reshape(512, 128) for s in some for q in range(4)],
+            axis=1,
+        )
+        if g is None:
+            rhs = [bd[s] for s in some]
+            places = [pl.ds(2 * q, 2) for q in range(4)]
         else:
-            src = co.at[s - 4]
-
-        lhs = jnp.concatenate(
-            [src[pl.ds(2 * q, 2), half[k], :].reshape(512, 128) for q in range(4)], axis=1
-        )
-        res = lax.dot_general(lhs, bd[s], (((1,), (1,)), ((), ())), preferred_element_type=F32)
-        for q in range(4):
-            acc[pl.ds(2 * q, 2), half[k], :] += res[:, q * 128:(q + 1) * 128].reshape(2, 256, 128)
-
-    byr.wait_recv()
-    piece = bbuf.at[three, pl.ds(4 * ((y + 3) % 4), 2)]
-    byr2 = put(piece, piece, d_yr)
-    byl.wait_recv()
-    piece = bbuf.at[three, pl.ds(4 * ((y + 1) % 4) + 2, 2)]
-    byl2 = put(piece, piece, d_yl)
-    f2 = spread(2)
+            at = [pl.ds(pl.multiple_of(256 * q + 128 * ((h + 1 - g) % 2), 128), 128) for q in range(2)]
+            rhs = [jnp.concatenate([bd[s, rows, :] for rows in at], axis=0) for s in some]
+            places = [cols(g, q) for q in range(2)]
+        res = lax.dot_general(
+            lhs, jnp.concatenate(rhs, axis=1), (((1,), (1,)), ((), ())), preferred_element_type=F32
+        )
+        for q, place in enumerate(places):
+            acc[place, half[k], :] += res[:, q * 128:(q + 1) * 128].reshape(2, 256, 128)
+
     alpha_dot(0, 0, True)
     alpha_dot(1, 0)
     alpha_dot(2, 0)
+    f3 = spread(3)
+    g00 = group_y(0, 0)
+    g01 = group_y(0, 1)
+    g10 = group_y(1, 0)
     for copy in m0 + m1:
         copy.wait_recv()
     alpha_dot(3, 0)
-    dr.wait_recv()
-    dl.wait_recv()
-    dr, dl = dstep(1, False)
     byr2.wait_recv()
     byl2.wait_recv()
     for s in range(8):
         fill_b(s)
-    for s in range(4):
-        beta_dot(s, 0)
-    f0[4].wait_recv()
-    f1[4].wait_recv()
+    n2 = across_x(2, f2)
     dr.wait_recv()
     dl.wait_recv()
     dr, dl = dstep(2, False)
-    beta_dot(4, 0)
+    beta_dot((0, 1), 0)
+    beta_dot((2, 3), 0)
+    n3 = across_x(3, f3)
+    r0 = group_right(0, g00)
+    l0 = group_left(0, g01)
+    g11 = group_y(1, 1)
+    f0[4].wait_recv()
+    f1[4].wait_recv()
     n0[2].wait_recv()
     n1[2].wait_recv()
-    beta_dot(5, 0)
-    beta_dot(6, 0)
-    n2 = across_x(2, f2)
+    beta_dot((4, 5), 0, 0)
     o0.wait_recv()
     o1.wait_recv()
-    beta_dot(7, 0)
-    alpha_dot(0, 1)
-    beta_dot(0, 1)
+    beta_dot((6, 7), 0, 0)
+    alpha_group(0, 0)
+    r1 = group_right(1, g10)
+    o2 = last_core(2, n2)
+    f2[4].wait_recv()
+    f3[4].wait_recv()
+    beta_dot((0, 4), 1, 0)
     dr.wait_recv()
     dl.wait_recv()
     dr, dl = dstep(3, True)
-    m2 = across_y(2, f2)
-    beta_dot(1, 1)
-    beta_dot(2, 1)
-    o2 = last_core(2, n2)
-    f2[4].wait_recv()
-    beta_dot(4, 1)
+    beta_dot((1, 2), 1, 0)
+    o3 = last_core(3, n3)
     n2[2].wait_recv()
-    beta_dot(5, 1)
-    beta_dot(6, 1)
-    beta_dot(3, 1)
-    alpha_dot(1, 1)
-    alpha_dot(2, 1)
+    n3[2].wait_recv()
+    beta_dot((5, 6), 1, 0)
+    g01[0].wait_recv()
+    alpha_group(1, 0)
+    g00[1].wait_recv()
+    alpha_group(2, 0)
+    r0.wait_recv()
+    l0.wait_recv()
+    alpha_group(3, 0)
     o2.wait_recv()
-    beta_dot(7, 1)
-    for copy in m2:
-        copy.wait_recv()
-    alpha_dot(3, 1)
-    dr.wait_recv()
-    dl.wait_recv()
+    o3.wait_recv()
+    beta_dot((3, 7), 1, 0)
 
     outs = []
-    for d in (4, 3, 5, 2, 6, 1, 7, 0):
-        zz = (z + d) % 8
-
+
+    def ready(zz):
         def finish(t, carry):
             rows = pl.ds(pl.multiple_of(t * 128, 128), 128)
             whole = acc[zz, rows] + dg[zz, rows] * ca[0, zz, rows].astype(F32)
@@ -333,10 +380,38 @@
             return carry
 
         lax.fori_loop(0, 4, finish, 0)
-        if d:
-            outs.append(put(sig.at[zz], out_ref.at[z], zdev(zz)))
-        else:
-            last = move(sig.at[zz], out_ref.at[zz])
+
+    def back(far_h, flip):
+        zz = 2 * ((h + far_h) % 4) + (1 - l if flip else l)
+        ready(zz)
+        outs.append(put(sig.at[zz], out_ref.at[z], zdev(zz)))
+
+    back(1, True)
+    back(3, True)
+    l1 = group_left(1, g11)
+    back(1, False)
+    back(3, False)
+    beta_dot((4, 5), 0, 1)
+    beta_dot((6, 7), 0, 1)
+    beta_dot((0, 4), 1, 1)
+    beta_dot((1, 2), 1, 1)
+    beta_dot((5, 6), 1, 1)
+    beta_dot((3, 7), 1, 1)
+    alpha_group(0, 1)
+    g11[0].wait_recv()
+    alpha_group(1, 1)
+    g10[1].wait_recv()
+    alpha_group(2, 1)
+    dr.wait_recv()
+    dl.wait_recv()
+    r1.wait_recv()
+    l1.wait_recv()
+    alpha_group(3, 1)
+    back(2, False)
+    back(2, True)
+    back(0, True)
+    ready(z)
+    last = move(sig.at[z], out_ref.at[z])
     last.wait()
     for copy in outs:
         copy.wait_recv()
@@ -344,20 +419,12 @@
         copy.wait_send()
 
 
-def slots(alpha_cols, beta_cols):
-    rows = jnp.arange(8)[:, None, None]
-    a = jnp.pad(alpha_cols, ((0, 4), (0, 0)))[:, None, :]
-    cols = jnp.where(rows == 4, beta_cols[None], a)
-    hit = cols == jnp.arange(128, dtype=jnp.int32)[None, :, None]
-    return jnp.min(jnp.where(hit, jnp.arange(16, dtype=jnp.int32), 16), axis=-1)
-
-
 def shards(ci_vectors, alpha_blocks, alpha_cols, beta_blocks, beta_cols, diagonal):
     hbm = pl.BlockSpec(memory_space=pltpu.MemorySpace.HBM)
     return pl.pallas_call(
         kernel,
         out_shape=jax.ShapeDtypeStruct((8, 512, 128), BF),
-        in_specs=[hbm] * 5,
+        in_specs=[hbm] * 6,
         out_specs=hbm,
         scratch_shapes=[
             pltpu.VMEM((4, 8, 512, 128), BF),
@@ -365,8 +432,11 @@
             pltpu.VMEM((4, 8, 512, 128), BF),
             pltpu.VMEM((8, 17, 128, 128), BF),
             pltpu.VMEM((4, 17, 128, 128), BF),
+            pltpu.VMEM((8, 128), jnp.int32),
             pltpu.VMEM((2, 8, 128), jnp.int32),
             pltpu.VMEM((4, 8, 128), jnp.int32),
+            pltpu.SMEM((4, 16), jnp.int32),
+            pltpu.SMEM((1, 16), jnp.int32),
             pltpu.SMEM((2, 8, 128), jnp.int32),
             pltpu.SMEM((4, 8, 128), jnp.int32),
             pltpu.VMEM((8, 512, 128), F32),
@@ -374,14 +444,14 @@
             pltpu.VMEM((8, 512, 512), BF),
             pltpu.VMEM((8, 512, 128), F32),
             pltpu.VMEM((8, 512, 128), BF),
-            pltpu.SemaphoreType.DMA((112,)),
-            pltpu.SemaphoreType.DMA((112,)),
+            pltpu.SemaphoreType.DMA((128,)),
+            pltpu.SemaphoreType.DMA((128,)),
             pltpu.SemaphoreType.DMA((16,)),
         ],
         compiler_params=pltpu.CompilerParams(
             collective_id=0, has_side_effects=True, vmem_limit_bytes=60 * 1024 * 1024
         ),
-    )(ci_vectors, alpha_blocks, beta_blocks, slots(alpha_cols, beta_cols), diagonal)
+    )(ci_vectors, alpha_blocks, alpha_cols, beta_blocks, beta_cols, diagonal)
 
 
 def solution(mesh):

time: 108 us -> 103 us (0.954); the launches traced: 107 us -> 101 us
  Pallas kernels: 104 us -> 98.8 us
  other arithmetic: 1.45 us -> 0 us
    pallas_call x1, Pallas kernels: 104 us -> 98.8 us  [shards(): pl.pallas_call(kernel, out_shape=jax.ShapeDtypeStruct((8, 512, 128), BF),...]
where the time goes in v3:
time: 103 us; the launch traced here: 101 us
  Pallas kernels  98.8 us (96%)
  local copies, waits for them, and re-layouts  2.27 us (2%)
    pallas_call x1, Pallas kernels, shards(): pl.pallas_call(kernel, out_shape=jax.ShapeDtypeStruct((8, 512, 128), BF),...  98.8 us
    unnamed x1, local copies, waits for them, and re-layouts  2.27 us

profile of v3, /device:TPU:1, one launch (start us, length us, event | category | flops | bytes accessed | tf_op | source)
XLA Modules:
  0.0 101.1 jit_solution(7599679880041982645)
XLA Ops:
  0.0 98.8 %shard_map.64 = bf16[8,512,128]{2,1,0:T(8,128)(2,1)} custom-call(bf16[8,512,128]{2,1,0:T(8,128)(2,1)} %c_ref.1, bf16[4,16,128,128]{3,2,1,0:T(8,128)(2,1)} %a_ref.1, s32[4,16]{1,0:T(4,128)} %ac_ref.1, bf16[1,16,128,128]{3,2,1,0:T(8,128)(2,1)} %b_ref.1, s32[1,16]{1,0:T(1,128)} %bc_ref.1, f32[512,128]{1,0:T(8,128)} %d_ref.1), custom_call_target="tpu_custom_call" | custom-call | tf_op jit(solution)/shard_map/pallas_call | solution.py:424
  98.8 2.3 %copy.8 = bf16[8,512,128]{2,1,0:T(8,128)(2,1)} copy(bf16[8,512,128]{2,1,0:T(8,128)(2,1)} %shard_map.64) | data formatting | bytes 2097152

commit v4 on v3

--- a/solution.py
+++ b/solution.py
@@ -12,7 +12,7 @@
 
 def kernel(
     c_ref, a_ref, ac_ref, b_ref, bc_ref, d_ref, out_ref,
-    ca, cs, co, abuf, bbuf, tab, ia, ib, sac, sbc, sa, sb, dg, ad, bd, acc, sig,
+    ca, cs, co, aown, aoth, bbuf, tab, ia, ib, sac, sbc, sown, soth, sb, dg, ad, bd, acc, sig,
     ss, rs, ls,
 ):
     i = lax.axis_index("alpha")
@@ -85,17 +85,17 @@
     turn(0)
     b1 = put(b_ref.at[0, quarter], bbuf.at[1, quarter], zdev(zout))
     turn(1)
-    a_in = put(a_ref.at[x, part], abuf.at[4 * l + x, part], zdev(jnp.where(c == 0, zin, zout)))
+    a_in = put(a_ref.at[x, part], aoth.at[x, part], zdev(jnp.where(c == 0, zin, zout)))
     own = [
-        move(a_ref.at[r], abuf.at[4 * l + r, pl.ds(0, 16)]) for r in range(4)
+        move(a_ref.at[r], aown.at[r, pl.ds(0, 16)]) for r in range(4)
     ] + [
         move(b_ref.at[0], bbuf.at[0, pl.ds(0, 16)]),
         move(d_ref, dg.at[z]),
     ]
     zero = jnp.zeros((128, 128), BF)
-    for r in range(8):
-        abuf[r, 16] = zero
     for r in range(4):
+        aown[r, 16] = zero
+        aoth[r, 16] = zero
         bbuf[r, 16] = zero
 
     cols_in[0].wait()
@@ -175,19 +175,52 @@
             put(dg.at[left], dg.at[left], zdev(zl)),
         )
 
+    ys = [y, (y + 3) % 4, (y + 1) % 4, (y + 2) % 4]
+
+    def fill_a(s, blocks, table, low):
+        def body(t, carry):
+            col = ((t // 2 % 2) * 4 + ys[s]) * 4 + (t // 4) * 2 + t % 2
+            for r in range(4):
+                at = table[r, col]
+                rows = pl.ds(pl.multiple_of(low * 512 + r * 128, 128), 128)
+                ad[s, rows, pl.ds(pl.multiple_of(t * 128, 128), 128)] = blocks[r, at]
+            return carry
+
+        lax.fori_loop(0, 8, body, 0)
+
+    def alpha_dot(some, low, fresh):
+        wide = jnp.concatenate(
+            [
+                jnp.concatenate(
+                    [ca[s, pl.ds(2 * q, 2), half[0]].reshape(512, 128) for q in range(4)], axis=1
+                )
+                for s in some
+            ],
+            axis=0,
+        )
+        rows = pl.ds(pl.multiple_of(low * 512, 512), 512)
+        lhs = jnp.concatenate([ad[s, rows, pl.ds(0, 512)] for s in some], axis=1)
+        res = jnp.dot(lhs, wide, preferred_element_type=F32)
+        for q in range(4):
+            piece = res[:, q * 128:(q + 1) * 128]
+            if fresh:
+                acc[2 * q + low] = piece
+            else:
+                acc[2 * q + low] += piece
+
     own_c.wait()
     f0 = spread(0)
     tb_in = [put(tab, ib.at[d], zdev((z + 8 + (2 * l - 1) * d) % 8)) for d in (3, 2, 1)]
-    ta_in = put(tab, ia.at[l], zdev(zin))
-    own += [move(tab, ia.at[l]), move(tab, ib.at[0])]
+    ta_in = put(tab, ia, zdev(zin))
+    tab_own = move(tab, sown)
+    own.append(move(tab, ib.at[0]))
     b1.wait_recv()
     b2 = put(bbuf.at[1, quarter], bbuf.at[2, quarter], zdev(zin))
     n0 = across_x(0, f0)
     m0 = across_y(0, f0)
     f1 = spread(1)
-    other = 4 * (1 - l)
     a_in.wait_recv()
-    piece = abuf.at[other + x, part]
+    piece = aoth.at[x, part]
     axr = put(piece, piece, d_xr)
     axl = put(piece, piece, d_xl)
     b2.wait_recv()
@@ -204,20 +237,26 @@
     byl = put(piece, piece, d_yl)
     n1 = across_x(1, f1)
     m1 = across_y(1, f1)
+    for copy in own[:4]:
+        copy.wait()
+    tab_own.wait()
+    for s in range(4):
+        fill_a(s, aown, sown, l)
     dr.wait_recv()
     dl.wait_recv()
     dr, dl = dstep(1, False)
     axr.wait_recv()
-    piece = abuf.at[other + (x + 3) % 4, pl.ds(8 * c, 4)]
+    piece = aoth.at[(x + 3) % 4, pl.ds(8 * c, 4)]
     axr2 = put(piece, piece, d_xr)
     axl.wait_recv()
-    piece = abuf.at[other + (x + 1) % 4, pl.ds(8 * c + 4, 4)]
+    piece = aoth.at[(x + 1) % 4, pl.ds(8 * c + 4, 4)]
     axl2 = put(piece, piece, d_xl)
+    alpha_dot((0, 1, 2), l, True)
     o1 = last_core(1, n1)
     f2 = spread(2)
     axr2.wait_recv()
     axl2.wait_recv()
-    piece = abuf.at[pl.ds(other, 4), part]
+    piece = aoth.at[pl.ds(0, 4), part]
     a_x = put(piece, piece, d_co)
     byr.wait_recv()
     piece = bbuf.at[three, pl.ds(4 * ((y + 3) % 4), 2)]
@@ -226,43 +265,16 @@
     piece = bbuf.at[three, pl.ds(4 * ((y + 1) % 4) + 2, 2)]
     byl2 = put(piece, piece, d_yl)
 
-    for copy in own:
+    for copy in own[4:]:
         copy.wait()
     ta_in.wait_recv()
     for copy in tb_in:
         copy.wait_recv()
-    ta_s = move(ia, sa)
+    ta_s = move(ia, soth)
     tb_s = move(ib, sb)
     ta_s.wait()
     tb_s.wait()
     a_x.wait_recv()
-    ys = [y, (y + 3) % 4, (y + 1) % 4, (y + 2) % 4]
-
-    def fill_a(s):
-        def body(t, carry):
-            col = ((t // 2 % 2) * 4 + ys[s]) * 4 + (t // 4) * 2 + t % 2
-            for r in range(8):
-                at = sa[r // 4, r % 4, col]
-                ad[s, pl.ds(r * 128, 128), pl.ds(pl.multiple_of(t * 128, 128), 128)] = abuf[r, at]
-            return carry
-
-        lax.fori_loop(0, 8, body, 0)
-
-    for s in range(4):
-        fill_a(s)
-
-    def alpha_dot(s, k, fresh=False):
-        wide = jnp.concatenate(
-            [ca[s, pl.ds(2 * q, 2), half[k]].reshape(512, 128) for q in range(4)], axis=1
-        )
-        res = jnp.dot(ad[s, :, pl.ds(512 * k, 512)], wide, preferred_element_type=F32)
-        for q in range(4):
-            piece = res[:, q * 128:(q + 1) * 128].reshape(2, 512, 128)
-            if fresh:
-                acc[pl.ds(2 * q, 2)] = piece
-            else:
-                acc[pl.ds(2 * q, 2)] += piece
-
     def alpha_group(s, g):
         wide = jnp.concatenate(
             [ca[s, cols(g, q), half[1]].reshape(512, 128) for q in range(2)], axis=1
@@ -313,16 +325,17 @@
         for q, place in enumerate(places):
             acc[place, half[k], :] += res[:, q * 128:(q + 1) * 128].reshape(2, 256, 128)
 
-    alpha_dot(0, 0, True)
-    alpha_dot(1, 0)
-    alpha_dot(2, 0)
+    for s in range(4):
+        fill_a(s, aoth, soth, 1 - l)
+    alpha_dot((0, 1, 2), 1 - l, True)
     f3 = spread(3)
     g00 = group_y(0, 0)
     g01 = group_y(0, 1)
     g10 = group_y(1, 0)
     for copy in m0 + m1:
         copy.wait_recv()
-    alpha_dot(3, 0)
+    alpha_dot((3,), l, False)
+    alpha_dot((3,), 1 - l, False)
     byr2.wait_recv()
     byl2.wait_recv()
     for s in range(8):
@@ -430,14 +443,16 @@
             pltpu.VMEM((4, 8, 512, 128), BF),
             pltpu.VMEM((3, 8, 512, 128), BF),
             pltpu.VMEM((4, 8, 512, 128), BF),
-            pltpu.VMEM((8, 17, 128, 128), BF),
+            pltpu.VMEM((4, 17, 128, 128), BF),
+            pltpu.VMEM((4, 17, 128, 128), BF),
             pltpu.VMEM((4, 17, 128, 128), BF),
             pltpu.VMEM((8, 128), jnp.int32),
-            pltpu.VMEM((2, 8, 128), jnp.int32),
+            pltpu.VMEM((8, 128), jnp.int32),
             pltpu.VMEM((4, 8, 128), jnp.int32),
             pltpu.SMEM((4, 16), jnp.int32),
             pltpu.SMEM((1, 16), jnp.int32),
-            pltpu.SMEM((2, 8, 128), jnp.int32),
+            pltpu.SMEM((8, 128), jnp.int32),
+            pltpu.SMEM((8, 128), jnp.int32),
             pltpu.SMEM((4, 8, 128), jnp.int32),
             pltpu.VMEM((8, 512, 128), F32),
             pltpu.VMEM((4, 1024, 1024), BF),

time: 103 us -> 101 us (0.981)
  Pallas kernels: 98.8 us -> 97.1 us
    pallas_call x1, Pallas kernels: 98.8 us -> 97.1 us  [shards(): pl.pallas_call(kernel, out_shape=jax.ShapeDtypeStruct((8, 512, 128), BF),...]
where the time goes in v4:
time: 101 us; the launch traced here: 99.4 us
  Pallas kernels  97.1 us (96%)
  local copies, waits for them, and re-layouts  2.27 us (2%)
    pallas_call x1, Pallas kernels, shards(): pl.pallas_call(kernel, out_shape=jax.ShapeDtypeStruct((8, 512, 128), BF),...  97.1 us
    unnamed x1, local copies, waits for them, and re-layouts  2.27 us

profile of v4, /device:TPU:1, one launch (start us, length us, event | category | flops | bytes accessed | tf_op | source)
XLA Modules:
  0.0 99.4 jit_solution(10278875963598646558)
XLA Ops:
  0.0 97.1 %shard_map.64 = bf16[8,512,128]{2,1,0:T(8,128)(2,1)} custom-call(bf16[8,512,128]{2,1,0:T(8,128)(2,1)} %c_ref.1, bf16[4,16,128,128]{3,2,1,0:T(8,128)(2,1)} %a_ref.1, s32[4,16]{1,0:T(4,128)} %ac_ref.1, bf16[1,16,128,128]{3,2,1,0:T(8,128)(2,1)} %b_ref.1, s32[1,16]{1,0:T(1,128)} %bc_ref.1, f32[512,128]{1,0:T(8,128)} %d_ref.1), custom_call_target="tpu_custom_call" | custom-call | tf_op jit(solution)/shard_map/pallas_call | solution.py:437
  97.1 2.3 %copy.8 = bf16[8,512,128]{2,1,0:T(8,128)(2,1)} copy(bf16[8,512,128]{2,1,0:T(8,128)(2,1)} %shard_map.64) | data formatting | bytes 2097152

commit v5 on v4

--- a/solution.py
+++ b/solution.py
@@ -345,11 +345,11 @@
     dl.wait_recv()
     dr, dl = dstep(2, False)
     beta_dot((0, 1), 0)
-    beta_dot((2, 3), 0)
-    n3 = across_x(3, f3)
     r0 = group_right(0, g00)
     l0 = group_left(0, g01)
     g11 = group_y(1, 1)
+    beta_dot((2, 3), 0)
+    n3 = across_x(3, f3)
     f0[4].wait_recv()
     f1[4].wait_recv()
     n0[2].wait_recv()

time: 101 us -> 100 us (0.990); the launches traced: 99.4 us -> 100 us
  no operation moved by 1% of the time
where the time goes in v5:
time: 100 us
  Pallas kernels  97.9 us (98%)
  local copies, waits for them, and re-layouts  2.27 us (2%)
    pallas_call x1, Pallas kernels, shards(): pl.pallas_call(kernel, out_shape=jax.ShapeDtypeStruct((8, 512, 128), BF),...  97.9 us
    unnamed x1, local copies, waits for them, and re-layouts  2.27 us

profile of v5, /device:TPU:1, one launch (start us, length us, event | category | flops | bytes accessed | tf_op | source)
XLA Modules:
  0.0 100.2 jit_solution(18107306090339658161)
XLA Ops:
  0.0 97.9 %shard_map.64 = bf16[8,512,128]{2,1,0:T(8,128)(2,1)} custom-call(bf16[8,512,128]{2,1,0:T(8,128)(2,1)} %c_ref.1, bf16[4,16,128,128]{3,2,1,0:T(8,128)(2,1)} %a_ref.1, s32[4,16]{1,0:T(4,128)} %ac_ref.1, bf16[1,16,128,128]{3,2,1,0:T(8,128)(2,1)} %b_ref.1, s32[1,16]{1,0:T(1,128)} %bc_ref.1, f32[512,128]{1,0:T(8,128)} %d_ref.1), custom_call_target="tpu_custom_call" | custom-call | tf_op jit(solution)/shard_map/pallas_call | solution.py:437
  97.9 2.3 %copy.8 = bf16[8,512,128]{2,1,0:T(8,128)(2,1)} copy(bf16[8,512,128]{2,1,0:T(8,128)(2,1)} %shard_map.64) | data formatting | bytes 2097152
